TPU v7x, 256 devices: a whole 4x4x8 slice. The times are simulated.
256 devices in a mesh: node: 64 (over z, x, core), feat: 4 (over y).
Axes of the slice: x: 4, y: 4, z: 8, core: 2. Of those that a mesh axis runs over, the one named last changes fastest.
Arguments:
- features: float32 [49152, 1024], P('node', 'feat'), may hold values from -6 to 6
- degrees: int32 [49152], P('node'), may hold values from 1 to 4
- tile_row: int32 [64, 201], P('node'), may hold values from 0 to 5, as said below
- tile_col: int32 [64, 201], P('node'), may hold values from 0 to 69, as said below
- tile_count: int32 [64], P('node'), may hold values from 75 to 201, as said below
- send_block: int32 [64, 64], replicated, may hold values from 0 to 5
- tile_val: bfloat16 [64, 201, 128, 128], P('node'), may hold values from -0.15625 to 0.15625
- weight: bfloat16 [1024, 3, 1024], P('node', None, 'feat'), may hold values from -0.109375 to 0.109375
- out_bias: float32 [1024], replicated, may hold values from -3 to 3
- cotangent: bfloat16 [49152, 1024], P(('node', 'feat')), may hold values from -0.109375 to 0.109375
Outputs:
- output: bfloat16 [49152, 1024], P(('node', 'feat'))
- weight_grad: float32 [1024, 3, 1024], P('node', None, 'feat')
- bias_grad: float32 [1024], replicated
Inputs may be any that keep to these rules, and one draw needn't show every extreme that they name: `tile_row`: the row block of each slot; for each other part q, between 1 and 3 live tiles of part p read slot 6 + q, each at a different row block. `tile_col`: below 6: the part's own row block; 6 + q: the block that part q sends; the first 12 slots of each part read own blocks, tile i < 6 at row block i, column i; slots past tile_count read 0; no tile reads slot 6 + p in part p. `tile_count`: live tiles come first in each part; some part has 201 live tiles.
All inputs are finite; a program needn't handle non-finite values.
Results may differ from a plain program's by a relative error of at most 0.0057.
Values may be sent and summed in bfloat16 or wider, within the bound.
No kernel may reach another device: no remote copies, remote signals or barrier semaphores. Data moves between devices by JAX's collectives and lax.ppermute only.
A program may use at most 192 MiB of HBM per device.

v0:
```python
import jax
import jax.numpy as jnp
from jax import lax
from jax.sharding import Mesh
from jax.sharding import PartitionSpec as P

HOPS = 2
NODE = ("node_0", "node_1", "node_2")
NODE_FEAT = ("node_0", "node_1", "node_2", "feat")


def sent_to_all(shard, axis):
    devices = lax.axis_size(axis)
    return lax.all_to_all(
        jnp.broadcast_to(shard[None], (devices, *shard.shape)), axis, 0, 0, tiled=True
    )


def laid_out(blocks, dim):
    dims = list(blocks.shape[1:])
    dims[dim] *= blocks.shape[0]
    return jnp.moveaxis(blocks, 0, dim).reshape(dims)


def collect(shard, axis, dim):
    blocks = sent_to_all(shard, axis)
    return laid_out(blocks, dim)


def split_up(shard, dim, devices):
    dims = shard.shape
    blocks = shard.reshape(*dims[:dim], devices, dims[dim] // devices, *dims[dim + 1 :])
    return jnp.moveaxis(blocks, dim, 0)


def sum_at_owner(shard, axis, dim):
    devices = lax.axis_size(axis)
    blocks = lax.all_to_all(split_up(shard, dim, devices), axis, 0, 0, tiled=True)
    return jnp.sum(blocks, axis=0)


def over_axes(shard, axes):
    for axis in axes:
        shard = lax.psum(shard, axis)
    return shard


def propagate(source, tile_rows, tile_cols, tile_values, is_live, send_row):
    block_size = tile_values.shape[-1]
    panel_width = source.shape[1]
    own_blocks = source.reshape(-1, block_size, panel_width)
    outgoing = own_blocks[send_row]
    arrived = lax.all_to_all(outgoing, NODE, split_axis=0, concat_axis=0, tiled=True)
    frame = jnp.concatenate([own_blocks, arrived], axis=0)
    sources = frame[tile_cols]
    product = jnp.einsum("tij,tjc->tic", tile_values, sources, preferred_element_type=jnp.float32)
    block_ids = jnp.arange(own_blocks.shape[0], dtype=jnp.int32)
    onehot = ((tile_rows[:, None] == block_ids[None, :]) & is_live[:, None]).astype(jnp.float32)
    summed = jnp.einsum("tr,tic->ric", onehot, product, precision=lax.Precision.HIGHEST)
    return summed.reshape(source.shape[0], panel_width)


def local(
    features,
    degrees,
    tile_row,
    tile_col,
    tile_count,
    send_block,
    tile_val,
    weight,
    out_bias,
    cotangent,
):
    node_index = lax.axis_index(NODE)
    send_row = lax.dynamic_index_in_dim(send_block, node_index, 0, keepdims=False)
    tile_rows = tile_row[0]
    tile_cols = tile_col[0]
    tile_values = tile_val[0]
    is_live = jnp.arange(tile_rows.shape[0], dtype=jnp.int32) < tile_count[0]
    row_scale = lax.rsqrt(degrees.astype(jnp.float32))[:, None]
    source = (features * row_scale).astype(jnp.bfloat16)
    hop_list = [features.astype(jnp.bfloat16)]
    for hop_number in range(HOPS):
        summed = propagate(source, tile_rows, tile_cols, tile_values, is_live, send_row)
        hop_list.append((summed * row_scale).astype(jnp.bfloat16))
        if hop_number + 1 < HOPS:
            source = (summed * row_scale * row_scale).astype(jnp.bfloat16)
    stacked = jnp.stack(hop_list, axis=1)
    hop_total = stacked.shape[1]
    flat_rows = stacked.reshape(stacked.shape[0], -1)
    piece = collect(weight, NODE, 0)
    flat_piece = piece.reshape(piece.shape[0], -1)
    panel_terms = lax.dot_general(
        flat_rows, flat_piece, (((1,), (1,)), ((), ())), preferred_element_type=jnp.float32
    )
    linear = sum_at_owner(panel_terms, "feat", 0)
    linear = linear + out_bias[None, :]
    sigmoid_val = jax.nn.sigmoid(linear)
    output = (linear * sigmoid_val).astype(jnp.bfloat16)
    grad_linear = (
        cotangent.astype(jnp.float32) * sigmoid_val * (1.0 + linear * (1.0 - sigmoid_val))
    ).astype(jnp.bfloat16)
    bias_grad = over_axes(jnp.sum(grad_linear.astype(jnp.float32), axis=0), NODE_FEAT)
    grad_all = collect(grad_linear, "feat", 0)
    term = lax.dot_general(
        grad_all, flat_rows, (((0,), (0,)), ((), ())), preferred_element_type=jnp.float32
    )
    weight_grad = sum_at_owner(
        term.reshape(weight.shape[0] * lax.axis_size(NODE), hop_total, -1), NODE, 0
    )
    return (output, weight_grad, bias_grad)


def solution(mesh):
    split = Mesh(
        mesh.devices.reshape(8, 4, 2, mesh.shape["feat"]), ("node_0", "node_1", "node_2", "feat")
    )
    return jax.shard_map(
        local,
        mesh=split,
        in_specs=(
            P(NODE, "feat"),
            P(NODE),
            P(NODE, None),
            P(NODE, None),
            P(NODE),
            P(),
            P(NODE, None, None, None),
            P(NODE, None, "feat"),
            P(),
            P(NODE_FEAT, None),
        ),
        out_specs=(P(NODE_FEAT, None), P(NODE, None, "feat"), P()),
        check_vma=False,
    )
```

profile of v0, /device:TPU:8, one launch (start us, length us, event | category | flops | bytes accessed | tf_op | source)
XLA Modules:
  0.0 572.4 jit_solution(15767024178187781781)
XLA Ops:
  2.0 2.3 convert_bitcast_fusion
  4.3 2.8 gather_fusion
  7.1 12.3 %all-to-all-start = ((bf16[64,128,256]{2,1,0:T(8,128)(2,1)}), bf16[64,128,256]{2,1,0:T(8,128)(2,1)}, u32[]{:S(2)}, u32[]{:S(2)}) async-start(bf16[64,128,256]{2,1,0:T(8,128)(2,1)} %gather_fusion), calls=%async_computation | async-start | bytes 8388608 | tf_op jit(solution)/shard_map/all_to_all | solution.py:53
  21.4 94.3 %all-to-all-done = bf16[64,128,256]{2,1,0:T(8,128)(2,1)} async-done(((bf16[64,128,256]{2,1,0:T(8,128)(2,1)}), bf16[64,128,256]{2,1,0:T(8,128)(2,1)}, u32[]{:S(2)}, u32[]{:S(2)}) %all-to-all-start) | async-done | bytes 4194336 | tf_op jit(solution)/shard_map/all_to_all | solution.py:53
  117.0 5.2 all-to-all-start.2
  122.2 4.6 pad_maximum_fusion
  126.9 10.9 %gather_fusion.1 = bf16[201,128,256]{2,1,0:T(8,128)(2,1)} fusion(bf16[70,128,256]{2,1,0:T(8,128)(2,1)} %pad_maximum_fusion, s32[1024]{0:T(1024)S(1)} %pad_clamp_fusion), kind=kCustom, calls=%fused_computation.1 | custom fusion | bytes 26346276 | tf_op jit(solution)/shard_map/gather | solution.py:55
  137.8 16.7 %convolution_bitcast_fusion.1 = f32[201,128,256]{1,2,0:T(8,128)} fusion(bf16[201,128,256]{2,1,0:T(8,128)(2,1)} %gather_fusion.1, bf16[1,201,128,128]{3,2,1,0:T(8,128)(2,1)} %param.16), kind=kOutput, calls=%fused_computation.5 | convolution fusion | flops 1686110208 | bytes 46104576 | tf_op jit(solution)/shard_map/tij,tjc->tic/dot_general | solution.py:56
  154.5 27.1 %copy.38 = f32[201,128,256]{2,0,1:T(8,128)} copy(f32[201,128,256]{1,2,0:T(8,128)} %convolution_bitcast_fusion.1) | data formatting | bytes 52690944 | tf_op jit(solution)/shard_map/tij,tjc->tic/dot_general | solution.py:56
  181.5 13.2 %multiply_convert_fusion = (bf16[6,128,256]{2,0,1:T(8,128)(2,1)S(1)}, f32[6,128,256]{2,0,1:T(8,128)S(1)}) fusion(f32[6,128]{0,1:T(8,128)S(1)} %copy-done.6, f32[201,128,256]{2,0,1:T(8,128)} %copy.38, s32[201]{0:T(256)S(1)} %bitcast.66, pred[201]{0:T(512)(128)(4,1)S(1)} %copy-done.10), kind=kOutput, calls=%fused_computation.13 | convolution fusion | flops 474810752 | bytes 27529196 | tf_op jit(solution)/shard_map/tr,tic->ric/dot_general | solution.py:59
  194.9 2.8 gather_fusion.2
  198.8 10.7 %all-to-all-start.1 = ((bf16[64,128,256]{2,1,0:T(8,128)(2,1)}), bf16[64,128,256]{2,1,0:T(8,128)(2,1)}, u32[]{:S(2)}, u32[]{:S(2)}) async-start(bf16[64,128,256]{2,1,0:T(8,128)(2,1)} %gather_fusion.2), calls=%async_computation.1 | async-start | bytes 8388608 | tf_op jit(solution)/shard_map/all_to_all | solution.py:53
  209.6 2.5 copy.47
  212.1 2.9 reshape.196
  215.2 90.5 %all-to-all-done.1 = bf16[64,128,256]{2,1,0:T(8,128)(2,1)} async-done(((bf16[64,128,256]{2,1,0:T(8,128)(2,1)}), bf16[64,128,256]{2,1,0:T(8,128)(2,1)}, u32[]{:S(2)}, u32[]{:S(2)}) %all-to-all-start.1) | async-done | bytes 4194336 | tf_op jit(solution)/shard_map/all_to_all | solution.py:53
  305.7 4.6 pad_maximum_fusion.1
  310.3 10.9 %gather_fusion.3 = bf16[201,128,256]{2,1,0:T(8,128)(2,1)} fusion(bf16[70,128,256]{2,1,0:T(8,128)(2,1)} %pad_maximum_fusion.1, s32[1024]{0:T(1024)S(1)} %pad_clamp_fusion), kind=kCustom, calls=%fused_computation.3 | custom fusion | bytes 26346276 | tf_op jit(solution)/shard_map/gather | solution.py:55
  321.2 16.7 %convolution_bitcast_fusion = f32[201,128,256]{1,2,0:T(8,128)} fusion(bf16[201,128,256]{2,1,0:T(8,128)(2,1)} %gather_fusion.3, bf16[1,201,128,128]{3,2,1,0:T(8,128)(2,1)} %param.16), kind=kOutput, calls=%fused_computation.4 | convolution fusion | flops 1686110208 | bytes 46104576 | tf_op jit(solution)/shard_map/tij,tjc->tic/dot_general | solution.py:56
  337.9 27.0 %copy.44 = f32[201,128,256]{2,0,1:T(8,128)} copy(f32[201,128,256]{1,2,0:T(8,128)} %convolution_bitcast_fusion) | data formatting | bytes 52690944 | tf_op jit(solution)/shard_map/tij,tjc->tic/dot_general | solution.py:56
  364.9 13.2 %fusion.8 = f32[6,128,256]{2,0,1:T(8,128)S(1)} fusion(f32[201,128,256]{2,0,1:T(8,128)} %copy.44, s32[201]{0:T(256)S(1)} %bitcast.67, pred[201]{0:T(512)(128)(4,1)S(1)} %copy-done.11), kind=kOutput, calls=%fused_computation.27 | convolution fusion | flops 474220928 | bytes 27132908 | tf_op jit(solution)/shard_map/tr,tic->ric/dot_general | solution.py:59
  381.3 2.5 dot_general.38
  383.8 2.7 fusion.18
  386.5 39.5 %all_to_all.30 = f32[4,192,1024]{2,1,0:T(8,128)S(1)} all-to-all(f32[4,192,1024]{2,1,0:T(8,128)S(1)} %fusion.18), channel_id=1, replica_groups=mesh['node_0'=8,'node_1'=4,'node_2'=2,'feat'=4] {'feat'}, dimensions={0} | all-to-all | bytes 6291456 | tf_op jit(solution)/shard_map/all_to_all | solution.py:38
  427.2 2.4 convert_reduce_fusion
  430.9 5.0 all-to-all-start.4
  437.5 15.4 %all-to-all-done.4 = bf16[4,192,1024]{2,1,0:T(8,128)(2,1)S(1)} async-done(((bf16[4,192,1024]{2,1,0:T(8,128)(2,1)}), bf16[4,192,1024]{2,1,0:T(8,128)(2,1)S(1)}, u32[]{:S(2)}, u32[]{:S(2)}) %all-to-all-start.4) | async-done | bytes 1572896 | tf_op jit(solution)/shard_map/all_to_all | solution.py:14
  454.5 4.8 fusion.2
  459.3 9.0 %all-to-all-start.5 = ((f32[64,16,3,256]{3,1,2,0:T(8,128)}), f32[64,16,3,256]{3,1,2,0:T(8,128)S(1)}, u32[]{:S(2)}, u32[]{:S(2)}) async-start(f32[64,16,3,256]{3,1,2,0:T(8,128)} %fusion.2), calls=%async_computation.5 | async-start | bytes 6291456 | tf_op jit(solution)/shard_map/all_to_all | solution.py:38
  468.3 80.4 %psum.28 = f32[1024]{0:T(1024)S(1)} all-reduce(f32[1024]{0:T(1024)S(1)} %get-tuple-element.3), channel_id=1, replica_groups=mesh['node_0'=8,'node_1'=4,'node_2'=2,'feat'=4] {'node_0'}, use_global_device_ids=true, to_apply=%region_3.4 | all-reduce | flops 1024 | bytes 8192 | tf_op jit(solution)/shard_map/psum | solution.py:44
  548.7 10.7 %psum.29 = f32[1024]{0:T(1024)S(1)} all-reduce(f32[1024]{0:T(1024)S(1)} %psum.28), channel_id=1, replica_groups=mesh['node_0'=8,'node_1'=4,'node_2'=2,'feat'=4] {'node_1'}, use_global_device_ids=true, to_apply=%region_4.5 | all-reduce | flops 1024 | bytes 8192 | tf_op jit(solution)/shard_map/psum | solution.py:44
  559.4 2.5 psum.30
  561.9 9.7 %psum.31 = f32[1024]{0:T(1024)} all-reduce(f32[1024]{0:T(1024)S(1)} %psum.30), channel_id=1, replica_groups=mesh['node_0'=8,'node_1'=4,'node_2'=2,'feat'=4] {'feat'}, use_global_device_ids=true, to_apply=%region_6.7 | all-reduce | flops 1024 | bytes 8192 | tf_op jit(solution)/shard_map/psum | solution.py:44
  (47 shorter events, 15.2 us)
Async XLA Ops:
  7.1 14.2 %copy-start.12 = (s32[1,201]{1,0:T(1,128)S(1)}, s32[1,201]{1,0:T(1,128)}, u32[]{:S(2)}) copy-start(s32[1,201]{1,0:T(1,128)} %param.13) | copy-start | bytes 2416
  7.1 108.6 %copy-start.7 = (bf16[16,3,256]{2,0,1:T(8,128)(2,1)S(1)}, bf16[16,3,256]{2,0,1:T(8,128)(2,1)}, u32[]{:S(2)}) copy-start(bf16[16,3,256]{2,0,1:T(8,128)(2,1)} %param.17) | copy-start | bytes 73732
  7.1 108.6 %all-to-all-start = ((bf16[64,128,256]{2,1,0:T(8,128)(2,1)}), bf16[64,128,256]{2,1,0:T(8,128)(2,1)}, u32[]{:S(2)}, u32[]{:S(2)}) async-start(bf16[64,128,256]{2,1,0:T(8,128)(2,1)} %gather_fusion), calls=%async_computation | async-start | bytes 8388608 | tf_op jit(solution)/shard_map/all_to_all | solution.py:53
  117.0 80.6 %all-to-all-start.2 = ((bf16[64,16,3,256]{3,1,2,0:T(8,128)(2,1)}), bf16[64,16,3,256]{3,1,2,0:T(8,128)(2,1)S(1)}, u32[]{:S(2)}, u32[]{:S(2)}) async-start(bf16[64,16,3,256]{3,1,2,0:T(8,128)(2,1)} %broadcast_in_dim.4), calls=%async_computation.2 | async-start | bytes 3145728 | tf_op jit(solution)/shard_map/all_to_all | solution.py:14
  154.5 27.1 %copy-start.6 = (f32[6,128]{0,1:T(8,128)S(1)}, f32[6,128]{0,1:T(8,128)}, u32[]{:S(2)}) copy-start(f32[6,128]{0,1:T(8,128)} %copy.40) | copy-start | bytes 9220
  154.5 27.1 %copy-start.8 = (s32[1,201]{1,0:T(1,128)S(1)}, s32[1,201]{1,0:T(1,128)}, u32[]{:S(2)}) copy-start(s32[1,201]{1,0:T(1,128)} %param.12) | copy-start | bytes 2416
  154.5 27.1 %copy-start.10 = (pred[201]{0:T(512)(128)(4,1)S(1)}, pred[201]{0:T(512)(128)(4,1)}, u32[]{:S(2)}) copy-start(pred[201]{0:T(512)(128)(4,1)} %iota_compare_fusion.1) | copy-start | bytes 607
  197.6 1.2 copy-start.2
  198.8 106.9 %all-to-all-start.1 = ((bf16[64,128,256]{2,1,0:T(8,128)(2,1)}), bf16[64,128,256]{2,1,0:T(8,128)(2,1)}, u32[]{:S(2)}, u32[]{:S(2)}) async-start(bf16[64,128,256]{2,1,0:T(8,128)(2,1)} %gather_fusion.2), calls=%async_computation.1 | async-start | bytes 8388608 | tf_op jit(solution)/shard_map/all_to_all | solution.py:53
  337.9 27.0 %copy-start.11 = (pred[201]{0:T(512)(128)(4,1)S(1)}, pred[201]{0:T(512)(128)(4,1)}, u32[]{:S(2)}) copy-start(pred[201]{0:T(512)(128)(4,1)} %iota_compare_fusion.1) | copy-start | bytes 607
  378.1 1.0 copy-start.4
  378.6 5.2 copy-start.3
  379.3 1.0 copy-start
  386.5 40.7 %copy-start.5 = (bf16[192,1024]{1,0:T(8,128)(2,1)S(1)}, bf16[192,1024]{1,0:T(8,128)(2,1)}, u32[]{:S(2)}) copy-start(bf16[192,1024]{1,0:T(8,128)(2,1)} %param.19) | copy-start | bytes 1179652
  386.5 40.7 %copy-start.9 = (f32[1024]{0:T(1024)S(1)}, f32[1024]{0:T(1024)}, u32[]{:S(2)}) copy-start(f32[1024]{0:T(1024)} %param.18) | copy-start | bytes 12292
  427.2 8.7 %copy-start.1 = (bf16[768,3,256]{2,0,1:T(8,128)(2,1)S(1)}, bf16[768,3,256]{2,0,1:T(8,128)(2,1)}, u32[]{:S(2)}) copy-start(bf16[768,3,256]{2,0,1:T(8,128)(2,1)} %copy-done) | copy-start | bytes 3538948
  430.9 22.0 %all-to-all-start.4 = ((bf16[4,192,1024]{2,1,0:T(8,128)(2,1)}), bf16[4,192,1024]{2,1,0:T(8,128)(2,1)S(1)}, u32[]{:S(2)}, u32[]{:S(2)}) async-start(bf16[4,192,1024]{2,1,0:T(8,128)(2,1)} %broadcast_in_dim.5), calls=%async_computation.4 | async-start | bytes 3145728 | tf_op jit(solution)/shard_map/all_to_all | solution.py:14
  459.3 112.3 %all-to-all-start.5 = ((f32[64,16,3,256]{3,1,2,0:T(8,128)}), f32[64,16,3,256]{3,1,2,0:T(8,128)S(1)}, u32[]{:S(2)}, u32[]{:S(2)}) async-start(f32[64,16,3,256]{3,1,2,0:T(8,128)} %fusion.2), calls=%async_computation.5 | async-start | bytes 6291456 | tf_op jit(solution)/shard_map/all_to_all | solution.py:38
where the time goes:
time: 574 us; the launch traced here: 572 us
  waiting for transfers between devices  200 us (35%)
  blocking collectives  143 us (25%)
  local copies, waits for them, and re-layouts  100 us (17%)
  matrix products  67.3 us (12%)
  starting transfers between devices  42.3 us (7%)
  other arithmetic  18.2 us (3%)
    all_to_all x2, waiting for transfers between devices, propagate(): lax.all_to_all(outgoing, NODE, split_axis=0, concat_axis=0, tiled=True)  185 us
    psum x4, blocking collectives, over_axes(): shard = lax.psum(shard, axis)  103 us
    dot_general x2, local copies, waits for them, and re-layouts, propagate(): jnp.einsum('tij,tjc->tic', tile_values, sources, preferred_element_type=j...  54.1 us
    all_to_all x1, blocking collectives, sum_at_owner(): lax.all_to_all(split_up(shard, dim, devices), axis, 0, 0, tiled=True)  39.5 us
    dot_general x2, matrix products, propagate(): jnp.einsum('tij,tjc->tic', tile_values, sources, preferred_element_type=j...  33.4 us
    dot_general x2, matrix products, propagate(): jnp.einsum('tr,tic->ric', onehot, product, precision=lax.Precision.HIGHEST)  26.4 us
    all_to_all x2, starting transfers between devices, propagate(): lax.all_to_all(outgoing, NODE, split_axis=0, concat_axis=0, tiled=True)  23.1 us
    gather x2, local copies, waits for them, and re-layouts, propagate(): sources = frame[tile_cols]  21.8 us
  transfers between devices with their start and end apart: 5, of which 3 were waited for; matrix products, arithmetic and copies ran while one was open for 15% of the time, Pallas kernels for 0%

commit v1 on v0

--- a/solution.py
+++ b/solution.py
@@ -41,7 +41,8 @@
 
 def over_axes(shard, axes):
     for axis in axes:
-        shard = lax.psum(shard, axis)
+        terms = lax.all_gather(shard, axis)
+        shard = jnp.sum(terms, axis=0)
     return shard
 
 

time: 574 us -> 587 us (1.023)
  blocking collectives: 143 us -> 154 us
    all_gather x0 -> x4, blocking collectives: none -> 114 us  [over_axes(): terms = lax.all_gather(shard, axis)]
    psum x4 -> x0, blocking collectives: 103 us -> none  [over_axes(): shard = lax.psum(shard, axis)]
  transfers between devices with their start and end apart: 5 -> 5, of which waited for: 3 -> 3; matrix products, arithmetic and copies ran while one was open for 15% -> 14% of each run, Pallas kernels for 0% -> 0%
where the time goes in v1:
time: 587 us; the launch traced here: 584 us
  waiting for transfers between devices  200 us (34%)
  blocking collectives  154 us (26%)
  local copies, waits for them, and re-layouts  100 us (17%)
  matrix products  67.3 us (11%)
  starting transfers between devices  42.3 us (7%)
  other arithmetic  18.9 us (3%)
    all_to_all x2, waiting for transfers between devices, propagate(): lax.all_to_all(outgoing, NODE, split_axis=0, concat_axis=0, tiled=True)  185 us
    all_gather x4, blocking collectives, over_axes(): terms = lax.all_gather(shard, axis)  114 us
    dot_general x2, local copies, waits for them, and re-layouts, propagate(): jnp.einsum('tij,tjc->tic', tile_values, sources, preferred_element_type=j...  54.1 us
    all_to_all x1, blocking collectives, sum_at_owner(): lax.all_to_all(split_up(shard, dim, devices), axis, 0, 0, tiled=True)  39.5 us
    dot_general x2, matrix products, propagate(): jnp.einsum('tij,tjc->tic', tile_values, sources, preferred_element_type=j...  33.4 us
    dot_general x2, matrix products, propagate(): jnp.einsum('tr,tic->ric', onehot, product, precision=lax.Precision.HIGHEST)  26.4 us
    all_to_all x2, starting transfers between devices, propagate(): lax.all_to_all(outgoing, NODE, split_axis=0, concat_axis=0, tiled=True)  23.1 us
    gather x2, local copies, waits for them, and re-layouts, propagate(): sources = frame[tile_cols]  21.8 us
  transfers between devices with their start and end apart: 5, of which 3 were waited for; matrix products, arithmetic and copies ran while one was open for 14% of the time, Pallas kernels for 0%

profile of v1, /device:TPU:8, one launch (start us, length us, event | category | flops | bytes accessed | tf_op | source)
XLA Modules:
  0.0 584.3 jit_solution(17139122735311222749)
XLA Ops:
  2.0 2.3 convert_bitcast_fusion
  4.3 2.8 gather_fusion
  7.1 12.3 %all-to-all-start = ((bf16[64,128,256]{2,1,0:T(8,128)(2,1)}), bf16[64,128,256]{2,1,0:T(8,128)(2,1)}, u32[]{:S(2)}, u32[]{:S(2)}) async-start(bf16[64,128,256]{2,1,0:T(8,128)(2,1)} %gather_fusion), calls=%async_computation | async-start | bytes 8388608 | tf_op jit(solution)/shard_map/all_to_all | solution.py:54
  21.4 94.3 %all-to-all-done = bf16[64,128,256]{2,1,0:T(8,128)(2,1)} async-done(((bf16[64,128,256]{2,1,0:T(8,128)(2,1)}), bf16[64,128,256]{2,1,0:T(8,128)(2,1)}, u32[]{:S(2)}, u32[]{:S(2)}) %all-to-all-start) | async-done | bytes 4194336 | tf_op jit(solution)/shard_map/all_to_all | solution.py:54
  117.0 5.2 all-to-all-start.2
  122.2 4.6 pad_maximum_fusion
  126.9 10.9 %gather_fusion.1 = bf16[201,128,256]{2,1,0:T(8,128)(2,1)} fusion(bf16[70,128,256]{2,1,0:T(8,128)(2,1)} %pad_maximum_fusion, s32[1024]{0:T(1024)S(1)} %pad_clamp_fusion), kind=kCustom, calls=%fused_computation.1 | custom fusion | bytes 26346276 | tf_op jit(solution)/shard_map/gather | solution.py:56
  137.8 16.7 %convolution_bitcast_fusion.1 = f32[201,128,256]{1,2,0:T(8,128)} fusion(bf16[201,128,256]{2,1,0:T(8,128)(2,1)} %gather_fusion.1, bf16[1,201,128,128]{3,2,1,0:T(8,128)(2,1)} %param.16), kind=kOutput, calls=%fused_computation.5 | convolution fusion | flops 1686110208 | bytes 46104576 | tf_op jit(solution)/shard_map/tij,tjc->tic/dot_general | solution.py:57
  154.5 27.1 %copy.51 = f32[201,128,256]{2,0,1:T(8,128)} copy(f32[201,128,256]{1,2,0:T(8,128)} %convolution_bitcast_fusion.1) | data formatting | bytes 52690944 | tf_op jit(solution)/shard_map/tij,tjc->tic/dot_general | solution.py:57
  181.5 13.2 %multiply_convert_fusion = (bf16[6,128,256]{2,0,1:T(8,128)(2,1)S(1)}, f32[6,128,256]{2,0,1:T(8,128)S(1)}) fusion(f32[6,128]{0,1:T(8,128)S(1)} %copy-done.6, f32[201,128,256]{2,0,1:T(8,128)} %copy.51, s32[201]{0:T(256)S(1)} %bitcast.66, pred[201]{0:T(512)(128)(4,1)S(1)} %copy-done.10), kind=kOutput, calls=%fused_computation.13 | convolution fusion | flops 474810752 | bytes 27529196 | tf_op jit(solution)/shard_map/tr,tic->ric/dot_general | solution.py:60
  194.9 2.8 gather_fusion.2
  198.8 10.7 %all-to-all-start.1 = ((bf16[64,128,256]{2,1,0:T(8,128)(2,1)}), bf16[64,128,256]{2,1,0:T(8,128)(2,1)}, u32[]{:S(2)}, u32[]{:S(2)}) async-start(bf16[64,128,256]{2,1,0:T(8,128)(2,1)} %gather_fusion.2), calls=%async_computation.1 | async-start | bytes 8388608 | tf_op jit(solution)/shard_map/all_to_all | solution.py:54
  209.6 2.5 copy.60
  212.1 2.9 reshape.200
  215.2 90.5 %all-to-all-done.1 = bf16[64,128,256]{2,1,0:T(8,128)(2,1)} async-done(((bf16[64,128,256]{2,1,0:T(8,128)(2,1)}), bf16[64,128,256]{2,1,0:T(8,128)(2,1)}, u32[]{:S(2)}, u32[]{:S(2)}) %all-to-all-start.1) | async-done | bytes 4194336 | tf_op jit(solution)/shard_map/all_to_all | solution.py:54
  305.7 4.6 pad_maximum_fusion.1
  310.3 10.9 %gather_fusion.3 = bf16[201,128,256]{2,1,0:T(8,128)(2,1)} fusion(bf16[70,128,256]{2,1,0:T(8,128)(2,1)} %pad_maximum_fusion.1, s32[1024]{0:T(1024)S(1)} %pad_clamp_fusion), kind=kCustom, calls=%fused_computation.3 | custom fusion | bytes 26346276 | tf_op jit(solution)/shard_map/gather | solution.py:56
  321.2 16.7 %convolution_bitcast_fusion = f32[201,128,256]{1,2,0:T(8,128)} fusion(bf16[201,128,256]{2,1,0:T(8,128)(2,1)} %gather_fusion.3, bf16[1,201,128,128]{3,2,1,0:T(8,128)(2,1)} %param.16), kind=kOutput, calls=%fused_computation.4 | convolution fusion | flops 1686110208 | bytes 46104576 | tf_op jit(solution)/shard_map/tij,tjc->tic/dot_general | solution.py:57
  337.9 27.0 %copy.57 = f32[201,128,256]{2,0,1:T(8,128)} copy(f32[201,128,256]{1,2,0:T(8,128)} %convolution_bitcast_fusion) | data formatting | bytes 52690944 | tf_op jit(solution)/shard_map/tij,tjc->tic/dot_general | solution.py:57
  364.9 13.2 %fusion.8 = f32[6,128,256]{2,0,1:T(8,128)S(1)} fusion(f32[201,128,256]{2,0,1:T(8,128)} %copy.57, s32[201]{0:T(256)S(1)} %bitcast.67, pred[201]{0:T(512)(128)(4,1)S(1)} %copy-done.11), kind=kOutput, calls=%fused_computation.27 | convolution fusion | flops 474220928 | bytes 27132908 | tf_op jit(solution)/shard_map/tr,tic->ric/dot_general | solution.py:60
  381.3 2.5 dot_general.38
  383.8 2.7 fusion.18
  386.5 39.5 %all_to_all.30 = f32[4,192,1024]{2,1,0:T(8,128)S(1)} all-to-all(f32[4,192,1024]{2,1,0:T(8,128)S(1)} %fusion.18), channel_id=1, replica_groups=mesh['node_0'=8,'node_1'=4,'node_2'=2,'feat'=4] {'feat'}, dimensions={0} | all-to-all | bytes 6291456 | tf_op jit(solution)/shard_map/all_to_all | solution.py:38
  427.2 2.4 convert_reduce_fusion
  430.9 5.0 all-to-all-start.4
  437.5 15.4 %all-to-all-done.4 = bf16[4,192,1024]{2,1,0:T(8,128)(2,1)S(1)} async-done(((bf16[4,192,1024]{2,1,0:T(8,128)(2,1)}), bf16[4,192,1024]{2,1,0:T(8,128)(2,1)S(1)}, u32[]{:S(2)}, u32[]{:S(2)}) %all-to-all-start.4) | async-done | bytes 1572896 | tf_op jit(solution)/shard_map/all_to_all | solution.py:14
  454.5 4.8 fusion.2
  459.3 9.0 %all-to-all-start.5 = ((f32[64,16,3,256]{3,1,2,0:T(8,128)}), f32[64,16,3,256]{3,1,2,0:T(8,128)S(1)}, u32[]{:S(2)}, u32[]{:S(2)}) async-start(f32[64,16,3,256]{3,1,2,0:T(8,128)} %fusion.2), calls=%async_computation.5 | async-start | bytes 6291456 | tf_op jit(solution)/shard_map/all_to_all | solution.py:38
  468.3 88.9 %all-gather = f32[8192]{0:T(1024)S(1)} all-gather(f32[1024]{0:T(1024)S(1)} %get-tuple-element.3), channel_id=2, replica_groups=mesh['node_0'=8,'node_1'=4,'node_2'=2,'feat'=4] {'node_0'}, dimensions={0}, use_global_device_ids=true | all-gather | bytes 36864 | tf_op jit(solution)/shard_map/all_gather | solution.py:44
  557.2 12.3 %all-gather.1 = f32[4096]{0:T(1024)S(1)} all-gather(f32[1024]{0:T(1024)S(1)} %reduce_sum.66), channel_id=3, replica_groups=mesh['node_0'=8,'node_1'=4,'node_2'=2,'feat'=4] {'node_1'}, dimensions={0}, use_global_device_ids=true | all-gather | bytes 20480 | tf_op jit(solution)/shard_map/all_gather | solution.py:44
  569.6 1.8 all-gather.2
  571.5 11.4 %all-gather.3 = f32[4096]{0:T(1024)S(1)} all-gather(f32[1024]{0:T(1024)S(1)} %reduce_sum.68), channel_id=5, replica_groups=mesh['node_0'=8,'node_1'=4,'node_2'=2,'feat'=4] {'feat'}, dimensions={0}, use_global_device_ids=true | all-gather | bytes 20480 | tf_op jit(solution)/shard_map/all_gather | solution.py:44
  (55 shorter events, 15.9 us)
Async XLA Ops:
  7.1 14.2 %copy-start.12 = (s32[1,201]{1,0:T(1,128)S(1)}, s32[1,201]{1,0:T(1,128)}, u32[]{:S(2)}) copy-start(s32[1,201]{1,0:T(1,128)} %param.13) | copy-start | bytes 2416
  7.1 108.6 %copy-start.7 = (bf16[16,3,256]{2,0,1:T(8,128)(2,1)S(1)}, bf16[16,3,256]{2,0,1:T(8,128)(2,1)}, u32[]{:S(2)}) copy-start(bf16[16,3,256]{2,0,1:T(8,128)(2,1)} %param.17) | copy-start | bytes 73732
  7.1 108.6 %all-to-all-start = ((bf16[64,128,256]{2,1,0:T(8,128)(2,1)}), bf16[64,128,256]{2,1,0:T(8,128)(2,1)}, u32[]{:S(2)}, u32[]{:S(2)}) async-start(bf16[64,128,256]{2,1,0:T(8,128)(2,1)} %gather_fusion), calls=%async_computation | async-start | bytes 8388608 | tf_op jit(solution)/shard_map/all_to_all | solution.py:54
  117.0 80.6 %all-to-all-start.2 = ((bf16[64,16,3,256]{3,1,2,0:T(8,128)(2,1)}), bf16[64,16,3,256]{3,1,2,0:T(8,128)(2,1)S(1)}, u32[]{:S(2)}, u32[]{:S(2)}) async-start(bf16[64,16,3,256]{3,1,2,0:T(8,128)(2,1)} %broadcast_in_dim.4), calls=%async_computation.2 | async-start | bytes 3145728 | tf_op jit(solution)/shard_map/all_to_all | solution.py:14
  154.5 27.1 %copy-start.6 = (f32[6,128]{0,1:T(8,128)S(1)}, f32[6,128]{0,1:T(8,128)}, u32[]{:S(2)}) copy-start(f32[6,128]{0,1:T(8,128)} %copy.53) | copy-start | bytes 9220
  154.5 27.1 %copy-start.8 = (s32[1,201]{1,0:T(1,128)S(1)}, s32[1,201]{1,0:T(1,128)}, u32[]{:S(2)}) copy-start(s32[1,201]{1,0:T(1,128)} %param.12) | copy-start | bytes 2416
  154.5 27.1 %copy-start.10 = (pred[201]{0:T(512)(128)(4,1)S(1)}, pred[201]{0:T(512)(128)(4,1)}, u32[]{:S(2)}) copy-start(pred[201]{0:T(512)(128)(4,1)} %iota_compare_fusion.1) | copy-start | bytes 607
  197.6 1.2 copy-start.2
  198.8 106.9 %all-to-all-start.1 = ((bf16[64,128,256]{2,1,0:T(8,128)(2,1)}), bf16[64,128,256]{2,1,0:T(8,128)(2,1)}, u32[]{:S(2)}, u32[]{:S(2)}) async-start(bf16[64,128,256]{2,1,0:T(8,128)(2,1)} %gather_fusion.2), calls=%async_computation.1 | async-start | bytes 8388608 | tf_op jit(solution)/shard_map/all_to_all | solution.py:54
  337.9 27.0 %copy-start.11 = (pred[201]{0:T(512)(128)(4,1)S(1)}, pred[201]{0:T(512)(128)(4,1)}, u32[]{:S(2)}) copy-start(pred[201]{0:T(512)(128)(4,1)} %iota_compare_fusion.1) | copy-start | bytes 607
  378.1 1.0 copy-start.4
  378.6 5.2 copy-start.3
  379.3 1.0 copy-start
  386.5 40.7 %copy-start.5 = (bf16[192,1024]{1,0:T(8,128)(2,1)S(1)}, bf16[192,1024]{1,0:T(8,128)(2,1)}, u32[]{:S(2)}) copy-start(bf16[192,1024]{1,0:T(8,128)(2,1)} %param.19) | copy-start | bytes 1179652
  386.5 40.7 %copy-start.9 = (f32[1024]{0:T(1024)S(1)}, f32[1024]{0:T(1024)}, u32[]{:S(2)}) copy-start(f32[1024]{0:T(1024)} %param.18) | copy-start | bytes 12292
  427.2 8.7 %copy-start.1 = (bf16[768,3,256]{2,0,1:T(8,128)(2,1)S(1)}, bf16[768,3,256]{2,0,1:T(8,128)(2,1)}, u32[]{:S(2)}) copy-start(bf16[768,3,256]{2,0,1:T(8,128)(2,1)} %copy-done) | copy-start | bytes 3538948
  430.9 22.0 %all-to-all-start.4 = ((bf16[4,192,1024]{2,1,0:T(8,128)(2,1)}), bf16[4,192,1024]{2,1,0:T(8,128)(2,1)S(1)}, u32[]{:S(2)}, u32[]{:S(2)}) async-start(bf16[4,192,1024]{2,1,0:T(8,128)(2,1)} %broadcast_in_dim.5), calls=%async_computation.4 | async-start | bytes 3145728 | tf_op jit(solution)/shard_map/all_to_all | solution.py:14
  459.3 124.2 %all-to-all-start.5 = ((f32[64,16,3,256]{3,1,2,0:T(8,128)}), f32[64,16,3,256]{3,1,2,0:T(8,128)S(1)}, u32[]{:S(2)}, u32[]{:S(2)}) async-start(f32[64,16,3,256]{3,1,2,0:T(8,128)} %fusion.2), calls=%async_computation.5 | async-start | bytes 6291456 | tf_op jit(solution)/shard_map/all_to_all | solution.py:38
